TPU v7x, 32 devices: a whole 2x2x4 slice. The times are simulated.
32 devices in a mesh: wrap: 8 (over z, y), samp: 4 (over x, core).
Axes of the slice: x: 2, y: 2, z: 4, core: 2. Of those that a mesh axis runs over, the one named last changes fastest.
Arguments:
- inputs: bfloat16 [4, 64, 64, 256], P('samp', None, 'wrap'), may hold values from -6 to 6
- cotangent: bfloat16 [4, 64, 64, 256], P('samp', None, 'wrap'), may hold values from -6 to 6
- weight_one: bfloat16 [64, 1728], replicated, may hold values from -0.15625 to 0.15625
- bias_one: float32 [64], replicated, may hold values from -3 to 3
- weight_two: bfloat16 [64, 1728], replicated, may hold values from -0.15625 to 0.15625
- bias_two: float32 [64], replicated, may hold values from -3 to 3
- dilation: int32 [2], replicated, may hold values from 1 to 4, as said below
Outputs:
- prediction: bfloat16 [4, 64, 64, 256], P('samp', None, 'wrap')
- grad_weight_one: float32 [64, 1728], replicated
- grad_bias_one: float32 [64], replicated
- grad_weight_two: float32 [64, 1728], replicated
- grad_bias_two: float32 [64], replicated
Inputs may be any that keep to these rules, and one draw needn't show every extreme that they name: `dilation`: in every draw one of the two rates equals 4.
All inputs are finite; a program needn't handle non-finite values.
Results may differ from a plain program's by a relative error of at most 0.006.
Values may be sent and summed in bfloat16 or wider, within the bound.
No kernel may reach another device: no remote copies, remote signals or barrier semaphores. Data moves between devices by JAX's collectives and lax.ppermute only.
A program may use at most 128 MiB of HBM per device.

v0:
```python
import math
import jax
import jax.numpy as jnp
from jax import lax
from jax.sharding import PartitionSpec as P

DMAX = 4
NR = 16
S = 16


def with_halo(x, sides, width):
    for axis, dim in sides:
        size, length = (lax.axis_size(axis), x.shape[dim])
        up = [(i, (i + 1) % size) for i in range(size)]
        down = [(j, i) for i, j in up]
        last = lax.slice_in_dim(x, length - width, length, axis=dim)
        initial = lax.slice_in_dim(x, 0, width, axis=dim)
        before = lax.ppermute(last, axis, up)
        after = lax.ppermute(initial, axis, down)
        x = jnp.concatenate([before, x, after], axis=dim)
    return x


def grid_of(field):
    chans = field.shape[0]
    shaped = field.reshape(chans, field.shape[1], NR, S)
    return jnp.pad(shaped, ((0, 0), (0, 0), (DMAX, DMAX), (DMAX, DMAX)))


def tap_stack(padded, rate, first_row, out_rows, tap_w):
    in_chan = padded.shape[0]
    anchor = jnp.zeros((), jnp.int32)
    windows = []
    for tap_n in range(3):
        for tap_s in range(3):
            offsets = (
                anchor,
                first_row + (tap_w - 1) * rate,
                DMAX + (tap_n - 1) * rate,
                DMAX + (tap_s - 1) * rate,
            )
            window = lax.dynamic_slice(padded, offsets, (in_chan, out_rows, NR, S))
            windows.append(window.reshape(in_chan, -1))
    return jnp.concatenate(windows, 0)


def convolve(padded, weight, rate, first_row, out_rows):
    in_chan = padded.shape[0]
    summed = None
    for tap_w in range(3):
        stacked = tap_stack(padded, rate, first_row, out_rows, tap_w)
        term = jnp.dot(
            weight[:, tap_w * 9 * in_chan : (tap_w + 1) * 9 * in_chan],
            stacked,
            preferred_element_type=jnp.float32,
        )
        summed = term if summed is None else summed + term
    return summed


def weight_grad(cot, padded, rate, first_row, out_rows):
    columns = []
    for tap_w in range(3):
        stacked = tap_stack(padded, rate, first_row, out_rows, tap_w)
        columns.append(
            lax.dot_general(
                cot, stacked, (((1,), (1,)), ((), ())), preferred_element_type=jnp.float32
            )
        )
    return jnp.concatenate(columns, 1)


def flip_kernel(weight):
    chans = weight.shape[0]
    shaped = weight.reshape(chans, 27, chans)[:, ::-1, :]
    return jnp.transpose(shaped, (2, 1, 0)).reshape(chans, 27 * chans)


def body(inputs, cotangent, weight_one, bias_one, weight_two, bias_two, dilation):
    samples_here = inputs.shape[0]
    chans = inputs.shape[1]
    rows = inputs.shape[2]
    first_rate = dilation[0]
    second_rate = dilation[1]
    factor = 1.0 / math.sqrt(
        samples_here * lax.axis_size("samp") * rows * lax.axis_size("wrap") * inputs.shape[3]
    )
    flipped = flip_kernel(weight_two)
    extended = with_halo(inputs, (("wrap", 2),), DMAX)
    sample = 0
    grid_in = grid_of(extended[sample])
    pre_one = convolve(grid_in, weight_one, first_rate, DMAX, rows) + bias_one[:, None]
    pre_list = [pre_one]
    hidden_list = [jax.nn.silu(pre_one).astype(jnp.bfloat16).reshape(chans, rows, -1)]
    grids = [grid_in]
    hidden_ext = with_halo(jnp.stack(hidden_list), (("wrap", 2),), DMAX)
    sample = 0
    hidden_grids = [grid_of(hidden_ext[sample])]
    input_first = DMAX
    grad_two = None
    bias_two_grad = None
    sample = 0
    output = (
        convolve(hidden_grids[sample], weight_two, second_rate, DMAX, rows) + bias_two[:, None]
    ).astype(jnp.bfloat16)
    outputs = [output.reshape(chans, rows, -1)]
    cot_flat = cotangent[sample].reshape(chans, -1)
    term = weight_grad(cot_flat, hidden_grids[sample], second_rate, DMAX, rows)
    bias_term = jnp.sum(cot_flat.astype(jnp.float32), 1)
    grad_two = term
    bias_two_grad = bias_term
    grad_two = grad_two * factor
    bias_two_grad = bias_two_grad * factor
    cot_ext = with_halo(cotangent, (("wrap", 2),), DMAX)
    grad_one = None
    bias_one_grad = None
    sample = 0
    back_hidden = convolve(grid_of(cot_ext[sample]), flipped, second_rate, DMAX, rows)
    pre_one = pre_list[sample]
    sigm = jax.nn.sigmoid(pre_one)
    back_pre = (back_hidden * sigm * (1.0 + pre_one * (1.0 - sigm))).astype(jnp.bfloat16)
    term = weight_grad(back_pre, grids[sample], first_rate, input_first, rows)
    bias_term = jnp.sum(back_pre.astype(jnp.float32), 1)
    grad_one = term
    bias_one_grad = bias_term
    grad_one = grad_one * factor
    bias_one_grad = bias_one_grad * factor
    grad_one, bias_one_grad, grad_two, bias_two_grad = lax.psum(
        (grad_one, bias_one_grad, grad_two, bias_two_grad), ("wrap", "samp")
    )
    return (jnp.stack(outputs), grad_one, bias_one_grad, grad_two, bias_two_grad)


def solution(mesh):
    in_specs = (
        P("samp", None, "wrap", None),
        P("samp", None, "wrap", None),
        P(),
        P(),
        P(),
        P(),
        P(),
    )
    out_specs = (P("samp", None, "wrap", None), P(), P(), P(), P())
    return jax.shard_map(body, mesh=mesh, in_specs=in_specs, out_specs=out_specs, check_vma=False)
```

profile of v0, /device:TPU:0, one launch (start us, length us, event | category | flops | bytes accessed | tf_op | source)
XLA Modules:
  0.0 347.6 jit_solution(2324225012075709310)
XLA Ops:
  7.2 1.3 copy.26
  9.3 3.0 collective-permute-start.4
  12.3 3.0 collective-permute-start.5
  15.4 1.3 copy.12
  16.8 4.7 %collective-permute-start.1 = (bf16[1,64,4,256]{1,3,2,0:T(8,128)(2,1)S(1)}, bf16[1,64,4,256]{1,3,2,0:T(8,128)(2,1)}, u32[]{:S(2)}, u32[]{:S(2)}) collective-permute-start(bf16[1,64,4,256]{1,3,2,0:T(8,128)(2,1)S(1)} %get-tuple-element.94), channel_id=1, source_target_pairs={{4,0},{8,4},{12,8},{16,12},{20,16},{24,20},{28,24},{0,28},{5,1},{9... | collective-permute-start | bytes 393224 | tf_op jit(solution)/shard_map/ppermute | solution.py:20
  31.1 1.7 collective-permute-done.5
  32.8 1.3 pad_maximum_fusion.1
  34.1 4.6 %pad_dynamic-slice_fusion = (bf16[64,8,16,16]{0,3,2,1:T(8,128)(2,1)}, bf16[64,8,16,16]{0,3,2,1:T(8,128)(2,1)}, bf16[64,8,16,16]{0,3,2,1:T(8,128)(2,1)}, bf16[64,...) fusion(s32[]{:T(128)S(6)} %select_n.23, ...), kind=kLoop, calls=%fused_computation | loop fusion | bytes 5505040 | tf_op jit(solution)/shard_map/dynamic_slice | solution.py:43
  38.7 4.6 %pad_dynamic-slice_fusion.1 = (bf16[64,8,16,16]{0,3,2,1:T(8,128)(2,1)}, bf16[64,8,16,16]{0,3,2,1:T(8,128)(2,1)}, bf16[64,8,16,16]{0,3,2,1:T(8,128)(2,1)}, bf16[6...) fusion(s32[]{:T(128)S(6)} %select_n.23, ...), kind=kLoop, calls=%fused_computation.1 | loop fusion | bytes 3670032 | tf_op jit(solution)/shard_map/dynamic_slice | solution.py:43
  43.3 1.3 pad_maximum_fusion
  44.6 4.6 %pad_dynamic-slice_fusion.26 = (bf16[64,8,16,16]{0,3,2,1:T(8,128)(2,1)}, bf16[64,8,16,16]{0,3,2,1:T(8,128)(2,1)}, bf16[64,8,16,16]{0,3,2,1:T(8,128)(2,1)}, bf16[...) fusion(s32[]{:T(128)S(6)} %select_n.19, ...), kind=kLoop, calls=%fused_computation.26 | loop fusion | bytes 5505040 | tf_op jit(solution)/shard_map/dynamic_slice | solution.py:43
  49.2 4.6 %pad_dynamic-slice_fusion.27 = (bf16[64,8,16,16]{0,3,2,1:T(8,128)(2,1)}, bf16[64,8,16,16]{0,3,2,1:T(8,128)(2,1)}, bf16[64,8,16,16]{0,3,2,1:T(8,128)(2,1)}, bf16[...) fusion(s32[]{:T(128)S(6)} %select_n.19, ...), kind=kLoop, calls=%fused_computation.27 | loop fusion | bytes 3670032 | tf_op jit(solution)/shard_map/dynamic_slice | solution.py:43
  53.8 5.2 %concatenate.67 = bf16[576,2048]{0,1:T(8,128)(2,1)S(1)} concatenate(bf16[64,2048]{0,1:T(8,128)(2,1)} %bitcast.166, bf16[64,2048]{0,1:T(8,128)(2,1)S(1)} %bitcast.163, bf16[64,2048]{0,1:T(8,128)(2,1)} %bitcast.212, bf16[64,2048]{0,1:T(8,128)(2,1)} %bitcast.164, bf16[64,2048]{0,1:T(8,128)(2,1)} %bitcast.165, bf16[64,2048]{0,1:T(8,128)(2,1)} %bitcast.211, ...), dimensions={0} | concatenate | bytes 4718592 | tf_op jit(solution)/shard_map/concatenate | solution.py:45
  59.0 1.8 fusion.17
  60.8 5.5 %concatenate.68 = bf16[576,2048]{0,1:T(8,128)(2,1)S(1)} concatenate(bf16[64,2048]{0,1:T(8,128)(2,1)} %bitcast.154, bf16[64,2048]{0,1:T(8,128)(2,1)} %bitcast.155, bf16[64,2048]{0,1:T(8,128)(2,1)} %bitcast.162, bf16[64,2048]{0,1:T(8,128)(2,1)} %bitcast.156, bf16[64,2048]{0,1:T(8,128)(2,1)} %bitcast.157, bf16[64,2048]{0,1:T(8,128)(2,1)} %bitcast.161, bf16[64,2048]{0,1:T(8,128)(2,1)} %bitcast.160, ...), dimensions={0} | concatenate | bytes 4718592 | tf_op jit(solution)/shard_map/concatenate | solution.py:45
  66.3 2.6 convolution_add_fusion.2
  69.0 5.3 %concatenate.56 = bf16[576,2048]{0,1:T(8,128)(2,1)S(1)} concatenate(bf16[64,2048]{0,1:T(8,128)(2,1)} %bitcast.190, bf16[64,2048]{0,1:T(8,128)(2,1)} %bitcast.187, bf16[64,2048]{0,1:T(8,128)(2,1)} %bitcast.224, bf16[64,2048]{0,1:T(8,128)(2,1)} %bitcast.188, bf16[64,2048]{0,1:T(8,128)(2,1)} %bitcast.189, bf16[64,2048]{0,1:T(8,128)(2,1)} %bitcast.223, bf16[64,2048]{0,1:T(8,128)(2,1)} %bitcast.222, ...), dimensions={0} | concatenate | bytes 4718592 | tf_op jit(solution)/shard_map/concatenate | solution.py:45
  74.3 1.8 fusion.26
  76.1 6.8 %concatenate.57 = bf16[576,2048]{0,1:T(8,128)(2,1)} concatenate(bf16[64,2048]{0,1:T(8,128)(2,1)} %bitcast.178, bf16[64,2048]{0,1:T(8,128)(2,1)} %bitcast.179, bf16[64,2048]{0,1:T(8,128)(2,1)} %bitcast.186, bf16[64,2048]{0,1:T(8,128)(2,1)} %bitcast.180, bf16[64,2048]{0,1:T(8,128)(2,1)} %bitcast.181, bf16[64,2048]{0,1:T(8,128)(2,1)} %bitcast.185, bf16[64,2048]{0,1:T(8,128)(2,1)} %bitcast.184, ...), dimensions={0} | concatenate | bytes 4718592 | tf_op jit(solution)/shard_map/concatenate | solution.py:45
  82.9 3.5 %convolution_add_fusion.4 = f32[2048,64]{0,1:T(8,128)} fusion(f32[2048,64]{0,1:T(8,128)S(1)} %fusion.26, bf16[576,2048]{0,1:T(8,128)(2,1)} %concatenate.57, bf16[64,1728]{1,0:T(8,128)(2,1)} %param.9), kind=kOutput, calls=%fused_computation.75 | convolution fusion | flops 151126016 | bytes 3751936 | tf_op jit(solution)/shard_map/dot_general | solution.py:53
  86.4 6.8 %concatenate.58 = bf16[576,2048]{0,1:T(8,128)(2,1)} concatenate(bf16[64,2048]{0,1:T(8,128)(2,1)} %bitcast.220, bf16[64,2048]{0,1:T(8,128)(2,1)} %bitcast.219, bf16[64,2048]{0,1:T(8,128)(2,1)} %bitcast.218, bf16[64,2048]{0,1:T(8,128)(2,1)} %bitcast.217, bf16[64,2048]{0,1:T(8,128)(2,1)} %bitcast.216, bf16[64,2048]{0,1:T(8,128)(2,1)} %bitcast.215, bf16[64,2048]{0,1:T(8,128)(2,1)} %bitcast.214, ...), dimensions={0} | concatenate | bytes 4718592 | tf_op jit(solution)/shard_map/concatenate | solution.py:45
  93.3 3.7 %multiply_convert_fusion = (bf16[64,2048]{1,0:T(8,128)(2,1)}, f32[64,2048]{1,0:T(8,128)}) fusion(f32[64]{0:T(128)S(1)} %copy-done.17, f32[2048,64]{0,1:T(8,128)} %convolution_add_fusion.4, bf16[576,2048]{0,1:T(8,128)(2,1)} %concatenate.58, bf16[64,1728]{1,0:T(8,128)(2,1)} %param.9), kind=kOutput, calls=%fused_computation.85 | convolution fusion | flops 151912448 | bytes 4014336 | tf_op jit(solution)/shard_map/dot_general | solution.py:53
  97.0 6.7 %concatenate.69 = bf16[576,2048]{0,1:T(8,128)(2,1)} concatenate(bf16[64,2048]{0,1:T(8,128)(2,1)} %bitcast.208, bf16[64,2048]{0,1:T(8,128)(2,1)} %bitcast.207, bf16[64,2048]{0,1:T(8,128)(2,1)} %bitcast.206, bf16[64,2048]{0,1:T(8,128)(2,1)} %bitcast.205, bf16[64,2048]{0,1:T(8,128)(2,1)} %bitcast.204, bf16[64,2048]{0,1:T(8,128)(2,1)} %bitcast.203, bf16[64,2048]{0,1:T(8,128)(2,1)} %bitcast.202, ...), dimensions={0} | concatenate | bytes 4718592 | tf_op jit(solution)/shard_map/concatenate | solution.py:45
  103.7 3.2 convert_reduce_fusion.1
  108.6 1.2 fusion.33
  111.7 4.5 %collective-permute-start.3 = (bf16[1,64,4,256]{1,3,2,0:T(8,128)(2,1)S(1)}, bf16[1,64,4,256]{1,3,2,0:T(8,128)(2,1)S(1)}, u32[]{:S(2)}, u32[]{:S(2)}) collective-permute-start(bf16[1,64,4,256]{1,3,2,0:T(8,128)(2,1)S(1)} %get-tuple-element.92), channel_id=1, source_target_pairs={{4,0},{8,4},{12,8},{16,12},{20,16},{24,20},{28,24},{0,28},{5,1},{9... | collective-permute-start | bytes 393224 | tf_op jit(solution)/shard_map/ppermute | solution.py:20
  116.2 1.9 concatenate.70
  118.0 40.3 %all-reduce.3 = (f32[64]{0:T(128)}, f32[64]{0:T(128)}) all-reduce(f32[64]{0:T(128)S(1)} %broadcast_multiply_fusion.3, f32[64]{0:T(128)S(1)} %broadcast_multiply_fusion.2), channel_id=1, replica_groups=mesh['wrap'=8,'samp'=4] {'wrap','samp'}, use_global_device_ids=true, to_apply=%region_2.3 | all-reduce | flops 128 | bytes 1024 | tf_op jit(solution)/shard_map/psum | solution.py:129
  158.4 2.6 select_maximum_fusion
  161.0 7.1 %constant_dynamic-slice_fusion.9 = (bf16[64,8,16,16]{0,3,2,1:T(8,128)(2,1)S(1)}, bf16[64,8,16,16]{0,3,2,1:T(8,128)(2,1)}, bf16[64,8,16,16]{0,3,2,1:T(8,128)(2,1)...) fusion(bf16[64,16,24,24]{0,3,2,1:T(8,128)(2,1)S(1)} %select_max, ...), kind=kLoop, calls=%fused_computation.120 | loop fusion | bytes 13631504 | tf_op jit(solution)/shard_map/dynamic_slice | solution.py:43
  170.0 1.9 copy.19
  171.9 1.9 copy.20
  173.9 2.0 copy.21
  178.8 2.3 copy.22
  181.1 1.9 copy.23
  183.0 1.9 copy.24
  185.9 5.3 %concatenate.63 = bf16[576,2048]{0,1:T(8,128)(2,1)S(1)} concatenate(bf16[64,2048]{0,1:T(8,128)(2,1)} %bitcast.200, bf16[64,2048]{0,1:T(8,128)(2,1)} %bitcast.199, bf16[64,2048]{0,1:T(8,128)(2,1)} %bitcast.198, bf16[64,2048]{0,1:T(8,128)(2,1)} %bitcast.197, bf16[64,2048]{0,1:T(8,128)(2,1)} %bitcast.196, bf16[64,2048]{0,1:T(8,128)(2,1)} %bitcast.195, bf16[64,2048]{0,1:T(8,128)(2,1)} %bitcast.194, ...), dimensions={0} | concatenate | bytes 4718592 | tf_op jit(solution)/shard_map/concatenate | solution.py:45
  191.2 1.8 fusion.22
  193.1 1.2 convolution_bitcast_fusion.1
  195.0 1.5 convolution_bitcast_fusion.2
  196.5 5.3 %concatenate.65 = bf16[576,2048]{0,1:T(8,128)(2,1)S(1)} concatenate(bf16[64,2048]{0,1:T(8,128)(2,1)} %bitcast.175, bf16[64,2048]{0,1:T(8,128)(2,1)} %bitcast.174, bf16[64,2048]{0,1:T(8,128)(2,1)} %bitcast.173, bf16[64,2048]{0,1:T(8,128)(2,1)} %bitcast.172, bf16[64,2048]{0,1:T(8,128)(2,1)} %bitcast.171, bf16[64,2048]{0,1:T(8,128)(2,1)} %bitcast.170, bf16[64,2048]{0,1:T(8,128)(2,1)} %bitcast.169, ...), dimensions={0} | concatenate | bytes 4718592 | tf_op jit(solution)/shard_map/concatenate | solution.py:45
  203.0 2.0 concatenate.71
  205.0 2.1 broadcast_multiply_fusion
  207.2 2.0 fusion.19
  209.1 1.5 fusion.13
  211.4 125.7 %all-reduce.7.cloned.1.call-done = (f32[64,1728]{1,0:T(8,128)}, f32[64,1728]{1,0:T(8,128)}) async-done(((f32[64,1728]{1,0:T(8,128)}, f32[64,1728]{1,0:T(8,128)}), (f32[64,1728]{1,0:T(8,128)}, f32[64,1728]{1,0:T(8,128)})) %all-reduce.7.cloned.1.call-update) | async-done | bytes 884752 | tf_op jit(solution)/shard_map/psum | solution.py:129
  337.1 1.8 copy.43
  338.9 1.8 copy.44
  (73 shorter events, 17.1 us)
Async XLA Ops:
  7.2 20.1 %copy-start.6 = (bf16[1,64,8,256]{3,2,1,0:T(8,128)(2,1)S(1)}, bf16[1,64,8,256]{3,2,1,0:T(8,128)(2,1)}, u32[]{:S(2)}) copy-start(bf16[1,64,8,256]{3,2,1,0:T(8,128)(2,1)} %param.8) | copy-start | bytes 786436
  7.2 14.3 %copy-start.15 = (s32[2]{0:T(128)S(1)}, s32[2]{0:T(128)}, u32[]{:S(2)}) copy-start(s32[2]{0:T(128)} %param.13) | copy-start | bytes 28
  7.2 20.6 %copy-start.14 = (bf16[64,1728]{1,0:T(8,128)(2,1)S(1)}, bf16[64,1728]{1,0:T(8,128)(2,1)}, u32[]{:S(2)}) copy-start(bf16[64,1728]{1,0:T(8,128)(2,1)} %param.11) | copy-start | bytes 663556
  7.2 329.9 %all-reduce.7.cloned.1.call-start = ((), (), s32[]{:S(2)}) async-start(), calls=%async_computation | async-start | bytes 1835008 | tf_op jit(solution)/shard_map/psum | solution.py:129
  9.3 21.8 %collective-permute-start.4 = (bf16[1,64,4,256]{1,3,2,0:T(8,128)(2,1)}, bf16[1,64,4,256]{1,3,2,0:T(8,128)(2,1)}, u32[]{:S(2)}, u32[]{:S(2)}) collective-permute-start(bf16[1,64,4,256]{1,3,2,0:T(8,128)(2,1)} %get-tuple-element.89), channel_id=1, source_target_pairs={{0,4},{4,8},{8,12},{12,16},{16,20},{20,24},{24,28},{28,0},{1,5},{5... | collective-permute-start | bytes 393224 | tf_op jit(solution)/shard_map/ppermute | solution.py:19
  12.3 20.5 %collective-permute-start.5 = (bf16[1,64,4,256]{1,3,2,0:T(8,128)(2,1)S(1)}, bf16[1,64,4,256]{1,3,2,0:T(8,128)(2,1)}, u32[]{:S(2)}, u32[]{:S(2)}) collective-permute-start(bf16[1,64,4,256]{1,3,2,0:T(8,128)(2,1)S(1)} %get-tuple-element.90), channel_id=1, source_target_pairs={{4,0},{8,4},{12,8},{16,12},{20,16},{24,20},{28,24},{0,28},{5,1},{9... | collective-permute-start | bytes 393224 | tf_op jit(solution)/shard_map/ppermute | solution.py:20
  16.7 26.6 %collective-permute-start = (bf16[1,64,4,256]{1,3,2,0:T(8,128)(2,1)S(1)}, bf16[1,64,4,256]{1,3,2,0:T(8,128)(2,1)}, u32[]{:S(2)}, u32[]{:S(2)}) collective-permute-start(bf16[1,64,4,256]{1,3,2,0:T(8,128)(2,1)S(1)} %get-tuple-element.93), channel_id=1, source_target_pairs={{0,4},{4,8},{8,12},{12,16},{16,20},{20,24},{24,28},{28,0},{1,5},{5... | collective-permute-start | bytes 393224 | tf_op jit(solution)/shard_map/ppermute | solution.py:19
  16.8 26.6 %collective-permute-start.1 = (bf16[1,64,4,256]{1,3,2,0:T(8,128)(2,1)S(1)}, bf16[1,64,4,256]{1,3,2,0:T(8,128)(2,1)}, u32[]{:S(2)}, u32[]{:S(2)}) collective-permute-start(bf16[1,64,4,256]{1,3,2,0:T(8,128)(2,1)S(1)} %get-tuple-element.94), channel_id=1, source_target_pairs={{4,0},{8,4},{12,8},{16,12},{20,16},{24,20},{28,24},{0,28},{5,1},{9... | collective-permute-start | bytes 393224 | tf_op jit(solution)/shard_map/ppermute | solution.py:20
  49.2 4.6 %copy-start.8 = (bf16[64,8,16,16]{0,3,2,1:T(8,128)(2,1)S(1)}, bf16[64,8,16,16]{0,3,2,1:T(8,128)(2,1)}, u32[]{:S(2)}) copy-start(bf16[64,8,16,16]{0,3,2,1:T(8,128)(2,1)} %get-tuple-element.36) | copy-start | bytes 786436
  86.4 6.8 %copy-start.17 = (f32[64]{0:T(128)S(1)}, f32[64]{0:T(128)}, u32[]{:S(2)}) copy-start(f32[64]{0:T(128)} %param.10) | copy-start | bytes 772
  93.2 3.8 %copy-start.7 = (bf16[64,8,16,16]{0,3,2,1:T(8,128)(2,1)S(1)}, bf16[64,8,16,16]{0,3,2,1:T(8,128)(2,1)}, u32[]{:S(2)}) copy-start(bf16[64,8,16,16]{0,3,2,1:T(8,128)(2,1)} %get-tuple-element.35) | copy-start | bytes 786436
  103.7 3.2 copy-start.5
  106.9 1.8 copy-start
  108.6 2.4 copy-start.9
  111.4 47.0 %collective-permute-start.2 = (bf16[1,64,4,256]{1,3,2,0:T(8,128)(2,1)S(1)}, bf16[1,64,4,256]{1,3,2,0:T(8,128)(2,1)S(1)}, u32[]{:S(2)}, u32[]{:S(2)}) collective-permute-start(bf16[1,64,4,256]{1,3,2,0:T(8,128)(2,1)S(1)} %get-tuple-element.91), channel_id=1, source_target_pairs={{0,4},{4,8},{8,12},{12,16},{16,20},{20,24},{24,28},{28,0},{1,5},{5... | collective-permute-start | bytes 393224 | tf_op jit(solution)/shard_map/ppermute | solution.py:19
  111.7 46.7 %collective-permute-start.3 = (bf16[1,64,4,256]{1,3,2,0:T(8,128)(2,1)S(1)}, bf16[1,64,4,256]{1,3,2,0:T(8,128)(2,1)S(1)}, u32[]{:S(2)}, u32[]{:S(2)}) collective-permute-start(bf16[1,64,4,256]{1,3,2,0:T(8,128)(2,1)S(1)} %get-tuple-element.92), channel_id=1, source_target_pairs={{4,0},{8,4},{12,8},{16,12},{20,16},{24,20},{28,24},{0,28},{5,1},{9... | collective-permute-start | bytes 393224 | tf_op jit(solution)/shard_map/ppermute | solution.py:20
  178.8 7.1 %copy-start.1 = (bf16[576,2048]{1,0:T(8,128)(2,1)}, bf16[576,2048]{1,0:T(8,128)(2,1)S(1)}, u32[]{:S(2)}) copy-start(bf16[576,2048]{1,0:T(8,128)(2,1)S(1)} %constant_dynamic-update-slice_fusion.4) | copy-start | bytes 7077892
  191.2 3.1 copy-start.12
  193.1 1.7 copy-start.2
  193.1 1.7 copy-start.13
  193.1 1.8 copy-start.11
  193.1 1.8 copy-start.10
  195.0 1.5 copy-start.3
  207.1 2.0 copy-start.4
  207.1 2.0 copy-start.16
Sparse Core Ops, SparseCore 0:
  207.3 129.7 all-reduce.6
where the time goes:
time: 351 us; the launch traced here: 348 us
  waiting for transfers between devices  127 us (36%)
  local copies, waits for them, and re-layouts  108 us (31%)
  blocking collectives  40.3 us (11%)
  matrix products  28.9 us (8%)
  between operations  19.6 us (6%)
  starting transfers between devices  15.6 us (4%)
  other arithmetic  7.83 us (2%)
    psum x1, waiting for transfers between devices, body(): lax.psum((grad_one, bias_one_grad, grad_two, bias_two_grad), ('wrap', 'sa...  126 us
    concatenate x9, local copies, waits for them, and re-layouts, tap_stack(): return jnp.concatenate(windows, 0)  47 us
    psum x1, blocking collectives, body(): lax.psum((grad_one, bias_one_grad, grad_two, bias_two_grad), ('wrap', 'sa...  40.3 us
    dynamic_slice x5, local copies, waits for them, and re-layouts, tap_stack(): window = lax.dynamic_slice(padded, offsets, (in_chan, out_rows, NR, S))  25.5 us
    dot_general x9, matrix products, convolve(): jnp.dot(weight[:, tap_w * 9 * in_chan:(tap_w + 1) * 9 * in_chan], stacked...  22 us
    reshape x8, local copies, waits for them, and re-layouts, tap_stack(): windows.append(window.reshape(in_chan, -1))  13.8 us
    unnamed x50, local copies, waits for them, and re-layouts  12.8 us
    ppermute x3, starting transfers between devices, with_halo(): after = lax.ppermute(initial, axis, down)  12.3 us
  transfers between devices with their start and end apart: 7, of which 2 were waited for; matrix products, arithmetic and copies ran while one was open for 6% of the time, Pallas kernels for 0%

commit v1 on v0

--- a/solution.py
+++ b/solution.py
@@ -127,7 +127,7 @@
     grad_one = grad_one * factor
     bias_one_grad = bias_one_grad * factor
     grad_one, bias_one_grad, grad_two, bias_two_grad = lax.psum(
-        (grad_one, bias_one_grad, grad_two, bias_two_grad), ("wrap", "samp")
+        lax.psum((grad_one, bias_one_grad, grad_two, bias_two_grad), "wrap"), "samp"
     )
     return (jnp.stack(outputs), grad_one, bias_one_grad, grad_two, bias_two_grad)
 

time: 351 us -> 302 us (0.86)
  waiting for transfers between devices: 127 us -> 87.2 us
  blocking collectives: 40.3 us -> 25.9 us
  local copies, waits for them, and re-layouts: 108 us -> 112 us
    psum x1 -> x2, waiting for transfers between devices: 126 us -> 81.1 us  [the longest x1 47 us: body(): lax.psum((grad_one, bias_one_grad, grad_two, bias_two_grad), 'wrap')]
    psum x1 -> x2, blocking collectives: 40.3 us -> 25.9 us  [the longest x1 19.8 us: body(): lax.psum((grad_one, bias_one_grad, grad_two, bias_two_grad), 'wrap')]
    unnamed x50 -> x44, local copies, waits for them, and re-layouts: 12.8 us -> 15.3 us
  transfers between devices with their start and end apart: 7 -> 8, of which waited for: 2 -> 5; matrix products, arithmetic and copies ran while one was open for 6% -> 9% of each run, Pallas kernels for 0% -> 0%
where the time goes in v1:
time: 302 us; the launch traced here: 298 us
  local copies, waits for them, and re-layouts  112 us (37%)
  waiting for transfers between devices  87.2 us (29%)
  matrix products  29.6 us (10%)
  blocking collectives  25.9 us (9%)
  between operations  19.6 us (6%)
  starting transfers between devices  15.7 us (5%)
  other arithmetic  8.32 us (3%)
    psum x1, waiting for transfers between devices, body(): lax.psum((grad_one, bias_one_grad, grad_two, bias_two_grad), 'wrap')  47 us
    concatenate x9, local copies, waits for them, and re-layouts, tap_stack(): return jnp.concatenate(windows, 0)  46.9 us
    psum x1, waiting for transfers between devices, body(): lax.psum(lax.psum((grad_one, bias_one_grad, grad_two, bias_two_grad), 'wr...  34 us
    dynamic_slice x5, local copies, waits for them, and re-layouts, tap_stack(): window = lax.dynamic_slice(padded, offsets, (in_chan, out_rows, NR, S))  25.3 us
    dot_general x9, matrix products, convolve(): jnp.dot(weight[:, tap_w * 9 * in_chan:(tap_w + 1) * 9 * in_chan], stacked...  20.9 us
    psum x1, blocking collectives, body(): lax.psum((grad_one, bias_one_grad, grad_two, bias_two_grad), 'wrap')  19.8 us
    unnamed x44, local copies, waits for them, and re-layouts  15.3 us
    reshape x8, local copies, waits for them, and re-layouts, tap_stack(): windows.append(window.reshape(in_chan, -1))  14.7 us
  transfers between devices with their start and end apart: 8, of which 5 were waited for; matrix products, arithmetic and copies ran while one was open for 9% of the time, Pallas kernels for 0%

profile of v1, /device:TPU:0, one launch (start us, length us, event | category | flops | bytes accessed | tf_op | source)
XLA Modules:
  0.0 298.4 jit_solution(1199023042302809043)
XLA Ops:
  7.2 1.3 copy.26
  8.6 3.0 %collective-permute-start.4 = (bf16[1,64,4,256]{1,3,2,0:T(8,128)(2,1)S(1)}, bf16[1,64,4,256]{1,3,2,0:T(8,128)(2,1)}, u32[]{:S(2)}, u32[]{:S(2)}) collective-permute-start(bf16[1,64,4,256]{1,3,2,0:T(8,128)(2,1)S(1)} %get-tuple-element.93), channel_id=1, source_target_pairs={{0,4},{4,8},{8,12},{12,16},{16,20},{20,24},{24,28},{28,0},{1,5},{5... | collective-permute-start | bytes 393224 | tf_op jit(solution)/shard_map/ppermute | solution.py:19
  11.7 3.1 %collective-permute-start.5 = (bf16[1,64,4,256]{1,3,2,0:T(8,128)(2,1)S(1)}, bf16[1,64,4,256]{1,3,2,0:T(8,128)(2,1)}, u32[]{:S(2)}, u32[]{:S(2)}) collective-permute-start(bf16[1,64,4,256]{1,3,2,0:T(8,128)(2,1)S(1)} %get-tuple-element.94), channel_id=1, source_target_pairs={{4,0},{8,4},{12,8},{16,12},{20,16},{24,20},{28,24},{0,28},{5,1},{9... | collective-permute-start | bytes 393224 | tf_op jit(solution)/shard_map/ppermute | solution.py:20
  14.8 1.3 copy.12
  16.9 4.7 %collective-permute-start.1 = (bf16[1,64,4,256]{1,3,2,0:T(8,128)(2,1)}, bf16[1,64,4,256]{1,3,2,0:T(8,128)(2,1)}, u32[]{:S(2)}, u32[]{:S(2)}) collective-permute-start(bf16[1,64,4,256]{1,3,2,0:T(8,128)(2,1)} %get-tuple-element.98), channel_id=1, source_target_pairs={{4,0},{8,4},{12,8},{16,12},{20,16},{24,20},{28,24},{0,28},{5,1},{9... | collective-permute-start | bytes 393224 | tf_op jit(solution)/shard_map/ppermute | solution.py:20
  30.7 1.5 collective-permute-done.5
  33.4 4.7 %pad_dynamic-slice_fusion = (bf16[64,8,16,16]{0,3,2,1:T(8,128)(2,1)}, bf16[64,8,16,16]{0,3,2,1:T(8,128)(2,1)S(1)}, bf16[64,8,16,16]{0,3,2,1:T(8,128)(2,1)}, bf16...) fusion(s32[]{:T(128)S(6)} %select_n.23, ...), kind=kLoop, calls=%fused_computation | loop fusion | bytes 5505040 | tf_op jit(solution)/shard_map/dynamic_slice | solution.py:43
  38.2 4.5 %pad_dynamic-slice_fusion.1 = (bf16[64,8,16,16]{0,3,2,1:T(8,128)(2,1)}, bf16[64,8,16,16]{0,3,2,1:T(8,128)(2,1)}, bf16[64,8,16,16]{0,3,2,1:T(8,128)(2,1)}, bf16[6...) fusion(s32[]{:T(128)S(6)} %select_n.23, ...), kind=kLoop, calls=%fused_computation.1 | loop fusion | bytes 3670032 | tf_op jit(solution)/shard_map/dynamic_slice | solution.py:43
  42.6 1.3 pad_maximum_fusion
  43.9 4.6 %pad_dynamic-slice_fusion.26 = (bf16[64,8,16,16]{0,3,2,1:T(8,128)(2,1)}, bf16[64,8,16,16]{0,3,2,1:T(8,128)(2,1)}, bf16[64,8,16,16]{0,3,2,1:T(8,128)(2,1)}, bf16[...) fusion(s32[]{:T(128)S(6)} %select_n.19, ...), kind=kLoop, calls=%fused_computation.26 | loop fusion | bytes 5505040 | tf_op jit(solution)/shard_map/dynamic_slice | solution.py:43
  48.5 4.5 %pad_dynamic-slice_fusion.27 = (bf16[64,8,16,16]{0,3,2,1:T(8,128)(2,1)}, bf16[64,8,16,16]{0,3,2,1:T(8,128)(2,1)}, bf16[64,8,16,16]{0,3,2,1:T(8,128)(2,1)}, bf16[...) fusion(s32[]{:T(128)S(6)} %select_n.19, ...), kind=kLoop, calls=%fused_computation.27 | loop fusion | bytes 3670032 | tf_op jit(solution)/shard_map/dynamic_slice | solution.py:43
  53.0 5.2 %concatenate.67 = bf16[576,2048]{0,1:T(8,128)(2,1)S(1)} concatenate(bf16[64,2048]{0,1:T(8,128)(2,1)} %bitcast.166, bf16[64,2048]{0,1:T(8,128)(2,1)S(1)} %bitcast.163, bf16[64,2048]{0,1:T(8,128)(2,1)} %bitcast.212, bf16[64,2048]{0,1:T(8,128)(2,1)} %bitcast.164, bf16[64,2048]{0,1:T(8,128)(2,1)} %bitcast.165, bf16[64,2048]{0,1:T(8,128)(2,1)} %bitcast.211, ...), dimensions={0} | concatenate | bytes 4718592 | tf_op jit(solution)/shard_map/concatenate | solution.py:45
  58.3 1.8 fusion.17
  60.1 5.5 %concatenate.68 = bf16[576,2048]{0,1:T(8,128)(2,1)S(1)} concatenate(bf16[64,2048]{0,1:T(8,128)(2,1)} %bitcast.154, bf16[64,2048]{0,1:T(8,128)(2,1)} %bitcast.155, bf16[64,2048]{0,1:T(8,128)(2,1)} %bitcast.162, bf16[64,2048]{0,1:T(8,128)(2,1)} %bitcast.156, bf16[64,2048]{0,1:T(8,128)(2,1)} %bitcast.157, bf16[64,2048]{0,1:T(8,128)(2,1)} %bitcast.161, bf16[64,2048]{0,1:T(8,128)(2,1)} %bitcast.160, ...), dimensions={0} | concatenate | bytes 4718592 | tf_op jit(solution)/shard_map/concatenate | solution.py:45
  65.6 2.6 convolution_add_fusion.2
  68.2 5.3 %concatenate.56 = bf16[576,2048]{0,1:T(8,128)(2,1)S(1)} concatenate(bf16[64,2048]{0,1:T(8,128)(2,1)} %bitcast.199, bf16[64,2048]{0,1:T(8,128)(2,1)} %bitcast.196, bf16[64,2048]{0,1:T(8,128)(2,1)} %bitcast.224, bf16[64,2048]{0,1:T(8,128)(2,1)} %bitcast.197, bf16[64,2048]{0,1:T(8,128)(2,1)} %bitcast.198, bf16[64,2048]{0,1:T(8,128)(2,1)} %bitcast.223, bf16[64,2048]{0,1:T(8,128)(2,1)} %bitcast.222, ...), dimensions={0} | concatenate | bytes 4718592 | tf_op jit(solution)/shard_map/concatenate | solution.py:45
  73.5 1.8 fusion.26
  75.3 6.8 %concatenate.57 = bf16[576,2048]{0,1:T(8,128)(2,1)} concatenate(bf16[64,2048]{0,1:T(8,128)(2,1)} %bitcast.187, bf16[64,2048]{0,1:T(8,128)(2,1)} %bitcast.188, bf16[64,2048]{0,1:T(8,128)(2,1)} %bitcast.195, bf16[64,2048]{0,1:T(8,128)(2,1)} %bitcast.189, bf16[64,2048]{0,1:T(8,128)(2,1)} %bitcast.190, bf16[64,2048]{0,1:T(8,128)(2,1)} %bitcast.194, bf16[64,2048]{0,1:T(8,128)(2,1)} %bitcast.193, ...), dimensions={0} | concatenate | bytes 4718592 | tf_op jit(solution)/shard_map/concatenate | solution.py:45
  82.1 3.5 %convolution_add_fusion.4 = f32[2048,64]{0,1:T(8,128)} fusion(f32[2048,64]{0,1:T(8,128)S(1)} %fusion.26, bf16[576,2048]{0,1:T(8,128)(2,1)} %concatenate.57, bf16[64,1728]{1,0:T(8,128)(2,1)} %param.9), kind=kOutput, calls=%fused_computation.75 | convolution fusion | flops 151126016 | bytes 3751936 | tf_op jit(solution)/shard_map/dot_general | solution.py:53
  85.6 6.8 %concatenate.58 = bf16[576,2048]{0,1:T(8,128)(2,1)} concatenate(bf16[64,2048]{0,1:T(8,128)(2,1)} %bitcast.220, bf16[64,2048]{0,1:T(8,128)(2,1)} %bitcast.219, bf16[64,2048]{0,1:T(8,128)(2,1)} %bitcast.218, bf16[64,2048]{0,1:T(8,128)(2,1)} %bitcast.217, bf16[64,2048]{0,1:T(8,128)(2,1)} %bitcast.216, bf16[64,2048]{0,1:T(8,128)(2,1)} %bitcast.215, bf16[64,2048]{0,1:T(8,128)(2,1)} %bitcast.214, ...), dimensions={0} | concatenate | bytes 4718592 | tf_op jit(solution)/shard_map/concatenate | solution.py:45
  92.4 3.7 %multiply_convert_fusion = (bf16[64,2048]{1,0:T(8,128)(2,1)}, f32[64,2048]{1,0:T(8,128)}) fusion(f32[64]{0:T(128)S(1)} %copy-done.14, f32[2048,64]{0,1:T(8,128)} %convolution_add_fusion.4, bf16[576,2048]{0,1:T(8,128)(2,1)} %concatenate.58, bf16[64,1728]{1,0:T(8,128)(2,1)} %param.9), kind=kOutput, calls=%fused_computation.85 | convolution fusion | flops 151912448 | bytes 4014336 | tf_op jit(solution)/shard_map/dot_general | solution.py:53
  96.1 6.7 %concatenate.69 = bf16[576,2048]{0,1:T(8,128)(2,1)} concatenate(bf16[64,2048]{0,1:T(8,128)(2,1)} %bitcast.208, bf16[64,2048]{0,1:T(8,128)(2,1)} %bitcast.207, bf16[64,2048]{0,1:T(8,128)(2,1)} %bitcast.206, bf16[64,2048]{0,1:T(8,128)(2,1)} %bitcast.205, bf16[64,2048]{0,1:T(8,128)(2,1)} %bitcast.204, bf16[64,2048]{0,1:T(8,128)(2,1)} %bitcast.203, bf16[64,2048]{0,1:T(8,128)(2,1)} %bitcast.202, ...), dimensions={0} | concatenate | bytes 4718592 | tf_op jit(solution)/shard_map/concatenate | solution.py:45
  102.8 3.2 %convert_reduce_fusion.1 = (f32[64]{0:T(128)S(1)}, bf16[64,2048]{1,0:T(8,128)(2,1)S(1)}) fusion(f32[64,2048]{1,0:T(8,128)} %get-tuple-element.102, f32[2048,64]{0,1:T(8,128)} %convolution_add_fusion.2, bf16[576,2048]{0,1:T(8,128)(2,1)} %concatenate.69, bf16[64,1728]{1,0:T(8,128)(2,1)} %reshape.409), kind=kOutput, calls=%fused_computation.84 | convolution fusion | flops 152567744 | bytes 4014336 | tf_op jit(solution)/shard_map/dot_general | solution.py:53
  111.2 4.7 %collective-permute-start.3 = (bf16[1,64,4,256]{1,3,2,0:T(8,128)(2,1)}, bf16[1,64,4,256]{1,3,2,0:T(8,128)(2,1)}, u32[]{:S(2)}, u32[]{:S(2)}) collective-permute-start(bf16[1,64,4,256]{1,3,2,0:T(8,128)(2,1)} %get-tuple-element.96), channel_id=1, source_target_pairs={{4,0},{8,4},{12,8},{16,12},{20,16},{24,20},{28,24},{0,28},{5,1},{9... | collective-permute-start | bytes 393224 | tf_op jit(solution)/shard_map/ppermute | solution.py:20
  115.9 2.2 fusion.32
  118.1 2.0 concatenate.70
  121.0 3.6 %collective-permute-done.3 = bf16[1,64,4,256]{1,3,2,0:T(8,128)(2,1)} collective-permute-done((bf16[1,64,4,256]{1,3,2,0:T(8,128)(2,1)}, bf16[1,64,4,256]{1,3,2,0:T(8,128)(2,1)}, u32[]{:S(2)}, u32[]{:S(2)}) %collective-permute-start.3) | collective-permute-done | bytes 131104 | tf_op jit(solution)/shard_map/ppermute | solution.py:20
  124.6 3.2 %select_maximum_fusion = bf16[64,16,24,24]{0,3,2,1:T(8,128)(2,1)S(1)} fusion(bf16[64,4,16,16]{0,3,2,1:T(8,128)(2,1)} %bitcast.37, bf16[64,8,16,16]{0,3,2,1:T(8,128)(2,1)S(1)} %bitcast.148, bf16[64,4,16,16]{0,3,2,1:T(8,128)(2,1)} %bitcast.35), kind=kLoop, calls=%fused_computation.59 | loop fusion | flops 11206656 | bytes 1703936 | tf_op jit(solution)/shard_map/concatenate | solution.py:21
  127.9 7.0 %constant_dynamic-slice_fusion.9 = (bf16[64,8,16,16]{0,3,2,1:T(8,128)(2,1)}, bf16[64,8,16,16]{0,3,2,1:T(8,128)(2,1)S(1)}, bf16[64,8,16,16]{0,3,2,1:T(8,128)(2,1)...) fusion(bf16[64,16,24,24]{0,3,2,1:T(8,128)(2,1)S(1)} %select_max, ...), kind=kLoop, calls=%fused_computation.120 | loop fusion | bytes 13631504 | tf_op jit(solution)/shard_map/dynamic_slice | solution.py:43
  134.8 1.9 copy.18
  137.8 1.9 copy.19
  139.7 1.9 copy.20
  141.6 1.9 copy.21
  146.5 1.9 copy.22
  148.4 1.9 copy.23
  150.4 1.9 copy.24
  156.5 1.5 convolution_bitcast_fusion.2
  158.0 5.3 %concatenate.63 = bf16[576,2048]{0,1:T(8,128)(2,1)S(1)} concatenate(bf16[64,2048]{0,1:T(8,128)(2,1)} %bitcast.186, bf16[64,2048]{0,1:T(8,128)(2,1)} %bitcast.185, bf16[64,2048]{0,1:T(8,128)(2,1)} %bitcast.184, bf16[64,2048]{0,1:T(8,128)(2,1)} %bitcast.183, bf16[64,2048]{0,1:T(8,128)(2,1)} %bitcast.182, bf16[64,2048]{0,1:T(8,128)(2,1)} %bitcast.181, bf16[64,2048]{0,1:T(8,128)(2,1)} %bitcast.180, ...), dimensions={0} | concatenate | bytes 4718592 | tf_op jit(solution)/shard_map/concatenate | solution.py:45
  163.3 1.5 convolution_bitcast_fusion.1
  164.8 5.2 %concatenate.65 = bf16[576,2048]{0,1:T(8,128)(2,1)S(1)} concatenate(bf16[64,2048]{0,1:T(8,128)(2,1)} %bitcast.176, bf16[64,2048]{0,1:T(8,128)(2,1)} %bitcast.175, bf16[64,2048]{0,1:T(8,128)(2,1)} %bitcast.174, bf16[64,2048]{0,1:T(8,128)(2,1)} %bitcast.173, bf16[64,2048]{0,1:T(8,128)(2,1)} %bitcast.172, bf16[64,2048]{0,1:T(8,128)(2,1)} %bitcast.171, bf16[64,2048]{0,1:T(8,128)(2,1)} %bitcast.170, ...), dimensions={0} | concatenate | bytes 4718592 | tf_op jit(solution)/shard_map/concatenate | solution.py:45
  172.5 2.0 broadcast_multiply_fusion
  175.2 19.8 %all-reduce.3 = (f32[64]{0:T(128)S(1)}, f32[64]{0:T(128)S(1)}) all-reduce(f32[64]{0:T(128)S(1)} %broadcast_multiply_fusion.3, f32[64]{0:T(128)S(1)} %broadcast_multiply_fusion.2), channel_id=1, replica_groups=mesh['wrap'=8,'samp'=4] {'wrap'}, use_global_device_ids=true, to_apply=%region_3.4 | all-reduce | flops 128 | bytes 1024 | tf_op jit(solution)/shard_map/psum | solution.py:130
  195.0 6.2 %all-reduce.5 = (f32[64]{0:T(128)}, f32[64]{0:T(128)}) all-reduce(f32[64]{0:T(128)S(1)} %get-tuple-element.5, f32[64]{0:T(128)S(1)} %get-tuple-element.6), channel_id=1, replica_groups=mesh['wrap'=8,'samp'=4] {'samp'}, use_global_device_ids=true, to_apply=%region_4.5 | all-reduce | flops 128 | bytes 1024 | tf_op jit(solution)/shard_map/psum | solution.py:129
  201.1 2.7 fusion.22
  203.8 47.0 %all-reduce.10.cloned.1.call-done = (f32[64,1728]{1,0:T(8,128)}, f32[64,1728]{1,0:T(8,128)}) async-done(((f32[64,1728]{1,0:T(8,128)}, f32[64,1728]{1,0:T(8,128)}), (f32[64,1728]{1,0:T(8,128)}, f32[64,1728]{1,0:T(8,128)})) %all-reduce.10.cloned.1.call-update) | async-done | bytes 884752 | tf_op jit(solution)/shard_map/psum | solution.py:130
  253.9 34.0 %all-reduce.12.cloned.1.call-done = (f32[64,1728]{1,0:T(8,128)}, f32[64,1728]{1,0:T(8,128)}) async-done(((f32[64,1728]{1,0:T(8,128)}, f32[64,1728]{1,0:T(8,128)}), (f32[64,1728]{1,0:T(8,128)}, f32[64,1728]{1,0:T(8,128)})) %all-reduce.12.cloned.1.call-update) | async-done | bytes 884752 | tf_op jit(solution)/shard_map/psum | solution.py:129
  288.0 1.8 copy.45
  289.8 1.8 copy.46
  (71 shorter events, 26.4 us)
Async XLA Ops:
  7.2 14.4 %copy-start.12 = (s32[2]{0:T(128)S(1)}, s32[2]{0:T(128)}, u32[]{:S(2)}) copy-start(s32[2]{0:T(128)} %param.13) | copy-start | bytes 28
  7.2 20.2 %copy-start.10 = (bf16[64,1728]{1,0:T(8,128)(2,1)S(1)}, bf16[64,1728]{1,0:T(8,128)(2,1)}, u32[]{:S(2)}) copy-start(bf16[64,1728]{1,0:T(8,128)(2,1)} %param.11) | copy-start | bytes 663556
  7.2 243.7 %all-reduce.10.cloned.1.call-start = ((), (), s32[]{:S(2)}) async-start(), calls=%async_computation | async-start | bytes 1835008 | tf_op jit(solution)/shard_map/psum | solution.py:130
  8.6 22.0 %collective-permute-start.4 = (bf16[1,64,4,256]{1,3,2,0:T(8,128)(2,1)S(1)}, bf16[1,64,4,256]{1,3,2,0:T(8,128)(2,1)}, u32[]{:S(2)}, u32[]{:S(2)}) collective-permute-start(bf16[1,64,4,256]{1,3,2,0:T(8,128)(2,1)S(1)} %get-tuple-element.93), channel_id=1, source_target_pairs={{0,4},{4,8},{8,12},{12,16},{16,20},{20,24},{24,28},{28,0},{1,5},{5... | collective-permute-start | bytes 393224 | tf_op jit(solution)/shard_map/ppermute | solution.py:19
  11.7 20.5 %collective-permute-start.5 = (bf16[1,64,4,256]{1,3,2,0:T(8,128)(2,1)S(1)}, bf16[1,64,4,256]{1,3,2,0:T(8,128)(2,1)}, u32[]{:S(2)}, u32[]{:S(2)}) collective-permute-start(bf16[1,64,4,256]{1,3,2,0:T(8,128)(2,1)S(1)} %get-tuple-element.94), channel_id=1, source_target_pairs={{4,0},{8,4},{12,8},{16,12},{20,16},{24,20},{28,24},{0,28},{5,1},{9... | collective-permute-start | bytes 393224 | tf_op jit(solution)/shard_map/ppermute | solution.py:20
  16.0 14.6 %copy-start.6 = (bf16[1,64,8,256]{3,2,1,0:T(8,128)(2,1)S(1)}, bf16[1,64,8,256]{3,2,1,0:T(8,128)(2,1)}, u32[]{:S(2)}) copy-start(bf16[1,64,8,256]{3,2,1,0:T(8,128)(2,1)} %param.8) | copy-start | bytes 786436
  16.9 25.7 %collective-permute-start = (bf16[1,64,4,256]{1,3,2,0:T(8,128)(2,1)}, bf16[1,64,4,256]{1,3,2,0:T(8,128)(2,1)}, u32[]{:S(2)}, u32[]{:S(2)}) collective-permute-start(bf16[1,64,4,256]{1,3,2,0:T(8,128)(2,1)} %get-tuple-element.97), channel_id=1, source_target_pairs={{0,4},{4,8},{8,12},{12,16},{16,20},{20,24},{24,28},{28,0},{1,5},{5... | collective-permute-start | bytes 393224 | tf_op jit(solution)/shard_map/ppermute | solution.py:19
  16.9 25.7 %collective-permute-start.1 = (bf16[1,64,4,256]{1,3,2,0:T(8,128)(2,1)}, bf16[1,64,4,256]{1,3,2,0:T(8,128)(2,1)}, u32[]{:S(2)}, u32[]{:S(2)}) collective-permute-start(bf16[1,64,4,256]{1,3,2,0:T(8,128)(2,1)} %get-tuple-element.98), channel_id=1, source_target_pairs={{4,0},{8,4},{12,8},{16,12},{20,16},{24,20},{28,24},{0,28},{5,1},{9... | collective-permute-start | bytes 393224 | tf_op jit(solution)/shard_map/ppermute | solution.py:20
  85.6 6.8 %copy-start.14 = (f32[64]{0:T(128)S(1)}, f32[64]{0:T(128)}, u32[]{:S(2)}) copy-start(f32[64]{0:T(128)} %param.10) | copy-start | bytes 772
  92.4 3.7 %copy-start.8 = (bf16[64,8,16,16]{0,3,2,1:T(8,128)(2,1)S(1)}, bf16[64,8,16,16]{0,3,2,1:T(8,128)(2,1)}, u32[]{:S(2)}) copy-start(bf16[64,8,16,16]{0,3,2,1:T(8,128)(2,1)} %get-tuple-element.39) | copy-start | bytes 786436
  102.8 3.2 %copy-start.4 = (bf16[576,2048]{0,1:T(8,128)(2,1)S(1)}, bf16[576,2048]{0,1:T(8,128)(2,1)}, u32[]{:S(2)}) copy-start(bf16[576,2048]{0,1:T(8,128)(2,1)} %concatenate.58) | copy-start | bytes 7077892
  106.0 3.1 %copy-start.5 = (bf16[64,2048]{1,0:T(8,128)(2,1)}, bf16[64,2048]{1,0:T(8,128)(2,1)S(1)}, u32[]{:S(2)}) copy-start(bf16[64,2048]{1,0:T(8,128)(2,1)S(1)} %get-tuple-element.104) | copy-start | bytes 786436
  106.1 1.9 copy-start.1
  111.2 9.8 %collective-permute-start.2 = (bf16[1,64,4,256]{1,3,2,0:T(8,128)(2,1)}, bf16[1,64,4,256]{1,3,2,0:T(8,128)(2,1)}, u32[]{:S(2)}, u32[]{:S(2)}) collective-permute-start(bf16[1,64,4,256]{1,3,2,0:T(8,128)(2,1)} %get-tuple-element.95), channel_id=1, source_target_pairs={{0,4},{4,8},{8,12},{12,16},{16,20},{20,24},{24,28},{28,0},{1,5},{5... | collective-permute-start | bytes 393224 | tf_op jit(solution)/shard_map/ppermute | solution.py:19
  111.2 13.4 %collective-permute-start.3 = (bf16[1,64,4,256]{1,3,2,0:T(8,128)(2,1)}, bf16[1,64,4,256]{1,3,2,0:T(8,128)(2,1)}, u32[]{:S(2)}, u32[]{:S(2)}) collective-permute-start(bf16[1,64,4,256]{1,3,2,0:T(8,128)(2,1)} %get-tuple-element.96), channel_id=1, source_target_pairs={{4,0},{8,4},{12,8},{16,12},{20,16},{24,20},{28,24},{0,28},{5,1},{9... | collective-permute-start | bytes 393224 | tf_op jit(solution)/shard_map/ppermute | solution.py:20
  136.8 9.7 %copy-start.9 = (bf16[64,2048]{1,0:T(8,128)(2,1)S(1)}, bf16[64,2048]{1,0:T(8,128)(2,1)}, u32[]{:S(2)}) copy-start(bf16[64,2048]{1,0:T(8,128)(2,1)} %get-tuple-element.101) | copy-start | bytes 786436
  156.5 1.5 copy-start.2
  163.3 1.5 copy-start
  171.3 3.3 %copy-start.7 = (bf16[1,64,8,256]{3,2,1,0:T(8,128)(2,1)S(1)}, bf16[1,64,8,256]{3,2,1,0:T(8,128)(2,1)}, u32[]{:S(2)}) copy-start(bf16[1,64,8,256]{3,2,1,0:T(8,128)(2,1)} %param.8) | copy-start | bytes 786436
  174.6 113.4 %all-reduce.12.cloned.1.call-start = ((), (), s32[]{:S(2)}) async-start(), calls=%async_computation.1 | async-start | bytes 1835008 | tf_op jit(solution)/shard_map/psum | solution.py:129
  201.1 49.7 %copy-start.11 = (bf16[64,1728]{1,0:T(8,128)(2,1)S(1)}, bf16[64,1728]{1,0:T(8,128)(2,1)}, u32[]{:S(2)}) copy-start(bf16[64,1728]{1,0:T(8,128)(2,1)} %param.11) | copy-start | bytes 663556
  250.9 1.7 copy-start.3
  250.9 1.7 copy-start.13
Sparse Core Ops, SparseCore 0:
  174.7 76.1 all-reduce.9
  253.2 34.6 all-reduce.11
